TPU v7x, 256 devices: a whole 4x4x8 slice. The times are simulated.
256 devices in a mesh: stem: 8 (over z_lo, y), tm: 32 (over x, z_hi, core).
Axes of the slice: x: 4, y: 4, z: 8 (z_hi: 4, z_lo: 2; z = z_hi * 2 + z_lo), core: 2. Of those that a mesh axis runs over, the one named last changes fastest.
Arguments:
- frames: bfloat16 [8, 12288, 1024], P('stem', 'tm'), may hold values from -6 to 6
- timestep: int32 [8], replicated, may hold values from 0 to 49, as said below
- modulation: float32 [50, 6, 1024], replicated, may hold values from -3 to 3
- qkv_self: bfloat16 [1024, 1536], replicated, may hold values from -0.1875 to 0.1875
- out_self: bfloat16 [512, 1024], replicated, may hold values from -0.25 to 0.25
- qk_gain_self: float32 [2, 64], replicated, may hold values from 1.5 to 6
- qkv_cross: bfloat16 [1024, 1536], replicated, may hold values from -0.1875 to 0.1875
- out_cross: bfloat16 [512, 1024], replicated, may hold values from -0.25 to 0.25
- qk_gain_cross: float32 [2, 64], replicated, may hold values from 1.5 to 6
Outputs:
- layer_out: bfloat16 [8, 12288, 1024], P('stem', 'tm')
Inputs may be any that keep to these rules, and one draw needn't show every extreme that they name: The stems' timestep indices are distinct, and index 0 and index 49 are always among them.
All inputs are finite; a program needn't handle non-finite values.
Results may differ from a plain program's by a relative error of at most 0.015.
The roundings to bfloat16 on the way count: a program that leaves them out, or rounds other values in their place, can miss the bound.
Values may be sent and summed in bfloat16 or wider, within the bound.
A program may use at most 128 MiB of HBM per device.

v0:
```python
import jax
import jax.numpy as jnp
from jax import lax
from jax.sharding import PartitionSpec as P

D = 1024
H = 8
HD = 64
HALF = 256
EPS = 1e-06
NEG = -1e30


def padded_2(block, sides, width):
    for axis, dim in sides:
        count = lax.axis_size(axis)
        forward = [(i, i + 1) for i in range(count - 1)]
        backward = [(target, source) for source, target in forward]
        low = lax.ppermute(
            lax.slice_in_dim(block, block.shape[dim] - width, None, axis=dim), axis, forward
        )
        high = lax.ppermute(lax.slice_in_dim(block, 0, width, axis=dim), axis, backward)
        block = jnp.concatenate([low, block, high], axis=dim)
    return block


def rounded(values):
    return lax.optimization_barrier(values.astype(jnp.bfloat16))


def layer_norm(values):
    values = values.astype(jnp.float32)
    centred = values - jnp.mean(values, axis=-1, keepdims=True)
    return centred * lax.rsqrt(jnp.mean(centred * centred, axis=-1, keepdims=True) + EPS)


def modulate(values, shift, scale):
    return layer_norm(values) * (1.0 + scale) + shift


def head_norm(values, gain):
    shaped = values.reshape(values.shape[:-1] + (H, HD))
    return shaped * lax.rsqrt(jnp.mean(shaped * shaped, axis=-1, keepdims=True) + EPS) * gain


def split_heads(projected, gains):
    width = H * HD
    query = rounded(head_norm(projected[..., :width], gains[0]))
    keyset = rounded(head_norm(projected[..., width : 2 * width], gains[1]))
    valueset = rounded(projected[..., 2 * width :].reshape(projected.shape[:-1] + (H, HD)))
    return (query, keyset, valueset)


def softmax_rows(scores):
    top = jnp.max(scores, axis=-1, keepdims=True)
    raised = jnp.exp(scores - top)
    return rounded(raised / jnp.sum(raised, axis=-1, keepdims=True))


def window_attend(query, padded, offset, total):
    rows = query.shape[0]
    width = H * HD

    def one_block(index):
        start = index * rows
        k_block = padded[0].reshape(-1, H, HD)
        v_block = padded[1].reshape(-1, H, HD)
        scores = jnp.einsum(
            "qhd,khd->hqk", query, k_block, preferred_element_type=jnp.float32
        ) * HD ** (-0.5)
        q_pos = offset + start + jnp.arange(rows, dtype=jnp.int32)
        k_pos = offset + start - HALF + jnp.arange(rows + 2 * HALF, dtype=jnp.int32)
        keep = (
            (jnp.abs(q_pos[:, None] - k_pos[None, :]) <= HALF)
            & (k_pos[None, :] >= 0)
            & (k_pos[None, :] < total)
        )
        weights = softmax_rows(jnp.where(keep[None], scores, NEG))
        return jnp.einsum("hqk,khd->qhd", weights, v_block, preferred_element_type=jnp.float32)

    blocks = lax.map(one_block, jnp.arange(rows // rows, dtype=jnp.int32))
    return rounded(blocks.reshape(rows, width))


def on_device(
    frames,
    timestep,
    modulation,
    qkv_self,
    out_self,
    qk_gain_self,
    qkv_cross,
    out_cross,
    qk_gain_cross,
):
    stem_count = lax.axis_size("stem")
    time_count = lax.axis_size("tm")
    rows = frames.shape[1]
    width = H * HD
    steps_all = modulation.shape[0]
    picks = (timestep[:, None] == jnp.arange(steps_all, dtype=jnp.int32)[None, :]).astype(
        jnp.float32
    )
    table = jnp.dot(
        picks, modulation.reshape(steps_all, -1), precision=lax.Precision.HIGHEST
    ).reshape(stem_count, 6, D)
    own = lax.dynamic_index_in_dim(table, lax.axis_index("stem"), 0, keepdims=False)
    source = frames[0]
    normed_self = rounded(modulate(source, own[0], own[1]))
    projected = jnp.dot(normed_self, qkv_self, preferred_element_type=jnp.float32)
    query, keyset, valueset = split_heads(projected, qk_gain_self)
    stacked = jnp.stack([keyset.reshape(rows, width), valueset.reshape(rows, width)])
    padded = padded_2(stacked, (("tm", 1),), HALF)
    offset = lax.axis_index("tm") * rows
    attended = window_attend(query, padded, offset, rows * time_count)
    first = rounded(
        source.astype(jnp.float32)
        + own[2] * jnp.dot(attended, out_self, preferred_element_type=jnp.float32)
    )
    normed_cross = rounded(modulate(first, own[3], own[4]))
    projected_cross = jnp.dot(normed_cross, qkv_cross, preferred_element_type=jnp.float32)
    q_cross, k_cross, v_cross = split_heads(projected_cross, qk_gain_cross)
    pair = jnp.stack([k_cross.reshape(rows, width), v_cross.reshape(rows, width)])[None]
    every = lax.all_gather(pair, "stem", axis=0, tiled=True)
    k_all = every[:, 0].reshape(stem_count, rows, H, HD)
    v_all = every[:, 1].reshape(stem_count, rows, H, HD)
    scores = jnp.einsum(
        "fhd,tfhd->fht", q_cross, k_all, preferred_element_type=jnp.float32
    ) * HD ** (-0.5)
    weights = softmax_rows(scores)
    mixed = rounded(
        jnp.einsum("fht,tfhd->fhd", weights, v_all, preferred_element_type=jnp.float32)
    ).reshape(rows, width)
    cross_out = rounded(jnp.dot(mixed, out_cross, preferred_element_type=jnp.float32))
    result = (first.astype(jnp.float32) + own[5] * cross_out.astype(jnp.float32)).astype(
        jnp.bfloat16
    )
    return result[None]


def solution(mesh):
    return jax.shard_map(
        on_device,
        mesh=mesh,
        in_specs=(P("stem", "tm", None), P(), P(), P(), P(), P(), P(), P(), P()),
        out_specs=P("stem", "tm", None),
        check_vma=False,
    )
```

profile of v0, /device:TPU:1, one launch (start us, length us, event | category | flops | bytes accessed | tf_op | source)
XLA Modules:
  0.0 176.1 jit_solution(18192869161088181082)
XLA Ops:
  6.5 2.2 %copy.46 = f32[50,6,1024]{2,1,0:T(8,128)S(1)} copy(f32[50,6,1024]{2,0,1:T(8,128)} %param.11) | data formatting | bytes 2457600 | tf_op args[2]
  8.8 0.3 pad.10
  9.0 1.9 %copy.75 = f32[7,8,6,1024]{3,1,2,0:T(8,128)} copy(f32[7,8,6,1024]{3,2,1,0:T(8,128)S(1)} %bitcast.95) | data formatting | bytes 2752512
  10.9 2.9 %dot_general.34 = f32[6,1024,50]{1,0,2:T(8,128)} reshape(f32[6144,50]{0,1:T(8,128)} %bitcast.97) | data formatting | bytes 2457600 | tf_op jit(solution)/shard_map/dot_general | solution.py:104
  13.8 1.3 convert_reduce_fusion.1
  15.1 1.5 fusion.17
  16.6 2.6 %fusion.23 = f32[8,6,1024]{2,0,1:T(8,128)S(1)} fusion(f32[6,1024,50]{1,0,2:T(8,128)} %dot_general.34, s32[8]{0:T(128)S(1)} %copy-done.10), kind=kOutput, calls=%fused_computation.35 | convolution fusion | flops 29491600 | bytes 1425440 | tf_op jit(solution)/shard_map/dot_general | solution.py:104
  19.3 1.5 fusion.20
  20.8 1.4 fusion.52
  22.2 0.1 fusion.49
  22.3 0.1 slice.123
  22.4 0.5 copy-done.8
  22.9 0.3 copy.50
  23.1 0.1 multiply_reduce_fusion.4
  23.2 0.3 copy.48
  23.5 0.1 multiply_reduce_fusion.5
  23.6 0.3 multiply_convert_fusion.2
  24.0 0.2 copy.49
  24.2 0.1 fusion.34
  24.3 5.2 %collective-permute-start.1 = (bf16[2,256,512]{1,2,0:T(8,128)(2,1)S(1)}, bf16[2,256,512]{1,2,0:T(8,128)(2,1)S(1)}, u32[]{:S(2)}, u32[]{:S(2)}) collective-permute-start(bf16[2,256,512]{1,2,0:T(8,128)(2,1)S(1)} %get-tuple-element.29), channel_id=1, source_target_pairs={{1,0},{2,1},{3,2},{4,3},{5,4},{6,5},{7,6},{8,7},{9,8},{10,9},{11,1... | collective-permute-start | bytes 1572872 | tf_op jit(solution)/shard_map/ppermute | solution.py:22
  29.4 3.2 %collective-permute-start = (bf16[2,256,512]{1,2,0:T(8,128)(2,1)S(1)}, bf16[2,256,512]{1,2,0:T(8,128)(2,1)}, u32[]{:S(2)}, u32[]{:S(2)}) collective-permute-start(bf16[2,256,512]{1,2,0:T(8,128)(2,1)S(1)} %get-tuple-element.28), channel_id=1, source_target_pairs={{0,1},{1,2},{2,3},{3,4},{4,5},{5,6},{6,7},{7,8},{8,9},{9,10},{10,1... | collective-permute-start | bytes 1572872 | tf_op jit(solution)/shard_map/ppermute | solution.py:19
  32.7 0.6 slice_bitcast_fusion.1
  33.3 1.2 fusion.26
  34.6 8.5 %collective-permute-done.1 = bf16[2,256,512]{1,2,0:T(8,128)(2,1)S(1)} collective-permute-done((bf16[2,256,512]{1,2,0:T(8,128)(2,1)S(1)}, bf16[2,256,512]{1,2,0:T(8,128)(2,1)S(1)}, u32[]{:S(2)}, u32[]{:S(2)}) %collective-permute-start.1) | collective-permute-done | bytes 524320 | tf_op jit(solution)/shard_map/ppermute | solution.py:22
  43.0 1.2 pad_maximum_fusion
  44.3 0.0 copy-start.5
  44.3 1.1 fusion.50
  45.4 9.1 %fusion.51 = (f32[8,384]{1,0:T(8,128)S(1)}, f32[8,384,896]{2,1,0:T(8,128)}) fusion(pred[384,896]{1,0:T(8,128)(4,1)S(1)} %copy-done.5, bf16[384,8,64]{0,2,1:T(8,128)(2,1)S(1)} %get-tuple-element.42, bf16[896,8,64]{0,2,1:T(8,128)(2,1)} %bitcast.105), kind=kOutput, calls=%fused_computation.98 | convolution fusion | flops 363332480 | bytes 12677120 | tf_op jit(solution)/shard_map/while/body/eval_jaxpr/sub | solution.py:56
  54.5 5.0 %divide_convert_fusion = bf16[8,384,896]{2,1,0:T(8,128)(2,1)S(1)} fusion(f32[8,384,896]{2,1,0:T(8,128)} %get-tuple-element.41, f32[8,384]{1,0:T(8,128)S(1)} %get-tuple-element.40), kind=kLoop, calls=%fused_computation.3 | loop fusion | flops 5505024 | bytes 16527360 | tf_op jit(solution)/shard_map/while/body/eval_jaxpr/convert_element_type | solution.py:28
  59.6 1.9 %convolution_convert_fusion.1 = bf16[8,64,384]{2,1,0:T(8,128)(2,1)S(1)} fusion(bf16[896,8,64]{0,2,1:T(8,128)(2,1)S(1)} %bitcast.98, bf16[8,384,896]{2,1,0:T(8,128)(2,1)S(1)} %divide_convert_fusion), kind=kOutput, calls=%fused_computation.40 | convolution fusion | flops 352518144 | bytes 6815744 | tf_op jit(solution)/shard_map/while/body/eval_jaxpr/hqk,khd->qhd/dot_general | solution.py:79
  61.5 0.6 fusion.21
  62.1 0.0 copy-start.11
  62.1 0.2 convert_reduce_fusion
  62.3 0.3 fusion.13
  62.7 0.4 copy-done.2
  63.0 0.4 fusion.16
  63.4 0.9 copy-done.11
  64.3 1.4 fusion.53
  65.7 0.1 slice.122
  65.7 0.1 fusion.48
  65.9 0.2 copy.53
  66.1 0.3 copy.52
  66.4 0.1 multiply_reduce_fusion.2
  66.5 0.0 copy-done.7
  66.5 0.1 multiply_convert_fusion
  66.6 0.1 pad_maximum_fusion.1
  66.7 1.2 copy.54
  67.9 0.0 all-gather.3.cloned.1.call-update
  67.9 0.3 copy.51
  68.2 0.1 multiply_reduce_fusion.3
  68.3 0.3 copy-done.6
  68.6 0.1 multiply_convert_fusion.1
  68.7 0.9 convert.8
  69.7 79.1 %all-gather.3.cloned.1.call-done = bf16[16,384,512]{2,1,0:T(8,128)(2,1)} async-done(((bf16[2,384,512]{2,1,0:T(8,128)(2,1)}), bf16[16,384,512]{2,1,0:T(8,128)(2,1)}) %all-gather.3.cloned.1.call-update) | async-done | bytes 6291472 | tf_op jit(solution)/shard_map/all_gather | solution.py:124
  148.7 6.1 %fusion.47 = (bf16[8,1,384,512]{3,2,1,0:T(8,128)(2,1)}, bf16[8,1,384,512]{3,2,1,0:T(8,128)(2,1)}) fusion(bf16[8,2,384,512]{3,2,1,0:T(8,128)(2,1)} %bitcast.96), kind=kLoop, calls=%fused_computation.94 | loop fusion | bytes 12582912 | tf_op jit(solution)/shard_map/slice | solution.py:125
  154.8 3.4 %copy.71 = bf16[8,1,384,512]{2,3,0,1:T(8,128)(2,1)S(1)} copy(bf16[8,1,384,512]{3,2,1,0:T(8,128)(2,1)} %get-tuple-element.14) | data formatting | bytes 6291456
  158.3 4.6 %copy.70 = bf16[8,1,384,512]{2,3,0,1:T(8,128)(2,1)} copy(bf16[8,1,384,512]{3,2,1,0:T(8,128)(2,1)} %get-tuple-element.13) | data formatting | bytes 6291456
  162.9 3.1 %multiply_reduce_fusion.1 = f32[384,8,8]{0,1,2:T(8,128)S(1)} fusion(bf16[384,8,64,8]{0,2,1,3:T(8,128)(2,1)} %bitcast.94, f32[384,8,64]{0,2,1:T(8,128)} %convert.8), kind=kLoop, calls=%fused_computation.8 | loop fusion | flops 4694016 | bytes 4030464
  166.0 0.1 fusion.32
  166.1 0.8 multiply_reduce_fusion
  166.9 0.4 copy-done.13
  167.3 0.6 convolution_convert_fusion
  167.9 0.2 copy-done.3
  168.1 1.2 fusion.33
  (35 shorter events, 0.2 us)
Async XLA Ops:
  6.5 14.2 %copy-start = (bf16[1024,1536]{1,0:T(8,128)(2,1)S(1)}, bf16[1024,1536]{1,0:T(8,128)(2,1)}, u32[]{:S(2)}) copy-start(bf16[1024,1536]{1,0:T(8,128)(2,1)} %param.12) | copy-start | bytes 9437188
  6.5 142.2 %all-gather.3.cloned.1.call-start = ((), (), s32[]{:S(2)}) async-start(), calls=%async_computation | async-start | bytes 7077888 | tf_op jit(solution)/shard_map/all_gather | solution.py:124
  10.9 5.7 %copy-start.10 = (s32[8]{0:T(128)S(1)}, s32[8]{0:T(128)}, u32[]{:S(2)}) copy-start(s32[8]{0:T(128)} %param.10) | copy-start | bytes 100
  22.2 0.7 copy-start.8
  24.0 8.8 %copy-start.9 = (f32[2,64]{1,0:T(2,128)S(1)}, f32[2,64]{1,0:T(2,128)}, u32[]{:S(2)}) copy-start(f32[2,64]{1,0:T(2,128)} %param.17) | copy-start | bytes 1540
  24.3 18.8 %collective-permute-start.1 = (bf16[2,256,512]{1,2,0:T(8,128)(2,1)S(1)}, bf16[2,256,512]{1,2,0:T(8,128)(2,1)S(1)}, u32[]{:S(2)}, u32[]{:S(2)}) collective-permute-start(bf16[2,256,512]{1,2,0:T(8,128)(2,1)S(1)} %get-tuple-element.29), channel_id=1, source_target_pairs={{1,0},{2,1},{3,2},{4,3},{5,4},{6,5},{7,6},{8,7},{9,8},{10,9},{11,1... | collective-permute-start | bytes 1572872 | tf_op jit(solution)/shard_map/ppermute | solution.py:22
  29.4 13.6 %collective-permute-start = (bf16[2,256,512]{1,2,0:T(8,128)(2,1)S(1)}, bf16[2,256,512]{1,2,0:T(8,128)(2,1)}, u32[]{:S(2)}, u32[]{:S(2)}) collective-permute-start(bf16[2,256,512]{1,2,0:T(8,128)(2,1)S(1)} %get-tuple-element.28), channel_id=1, source_target_pairs={{0,1},{1,2},{2,3},{3,4},{4,5},{5,6},{6,7},{7,8},{8,9},{9,10},{10,1... | collective-permute-start | bytes 1572872 | tf_op jit(solution)/shard_map/ppermute | solution.py:19
  44.3 1.1 copy-start.5
  59.5 1.9 %copy-start.4 = (bf16[1,384,1024]{2,1,0:T(8,128)(2,1)S(1)}, bf16[1,384,1024]{2,1,0:T(8,128)(2,1)}, u32[]{:S(2)}) copy-start(bf16[1,384,1024]{2,1,0:T(8,128)(2,1)} %param.9) | copy-start | bytes 2359300
  59.6 1.9 %copy-start.12 = (bf16[512,1024]{1,0:T(8,128)(2,1)S(1)}, bf16[512,1024]{1,0:T(8,128)(2,1)}, u32[]{:S(2)}) copy-start(bf16[512,1024]{1,0:T(8,128)(2,1)} %param.13) | copy-start | bytes 3145732
  62.1 0.9 copy-start.2
  62.1 2.2 %copy-start.11 = (bf16[1024,1536]{1,0:T(8,128)(2,1)S(1)}, bf16[1024,1536]{1,0:T(8,128)(2,1)}, u32[]{:S(2)}) copy-start(bf16[1024,1536]{1,0:T(8,128)(2,1)} %param.15) | copy-start | bytes 9437188
  65.9 0.6 copy-start.7
  67.9 0.7 copy-start.6
  166.1 1.2 copy-start.13
  166.9 1.2 copy-start.3
  166.9 2.4 %copy-start.1 = (bf16[1024,1536]{1,0:T(8,128)(2,1)S(1)}, bf16[1024,1536]{1,0:T(8,128)(2,1)}, u32[]{:S(2)}) copy-start(bf16[1024,1536]{1,0:T(8,128)(2,1)} %param.12) | copy-start | bytes 9437188
Sparse Core Ops, SparseCore 0:
  68.1 80.6 all-gather.2
where the time goes:
time: 177 us; the launch traced here: 176 us
  waiting for transfers between devices  87.6 us (49%)
  local copies, waits for them, and re-layouts  28.8 us (16%)
  other arithmetic  19.9 us (11%)
  matrix products  17.6 us (10%)
  between operations  13.9 us (8%)
  starting transfers between devices  8.4 us (5%)
    all_gather x1, waiting for transfers between devices, on_device(): every = lax.all_gather(pair, 'stem', axis=0, tiled=True)  79.1 us
    unnamed x34, local copies, waits for them, and re-layouts  15.1 us
    sub x1, matrix products, softmax_rows(): raised = jnp.exp(scores - top)  9.13 us
    ppermute x1, waiting for transfers between devices, padded_2(): lax.ppermute(lax.slice_in_dim(block, 0, width, axis=dim), axis, backward)  8.48 us
    convert_element_type x6, other arithmetic, rounded(): return lax.optimization_barrier(values.astype(jnp.bfloat16))  7.51 us
    slice x1, local copies, waits for them, and re-layouts, on_device(): k_all = every[:, 0].reshape(stem_count, rows, H, HD)  6.06 us
    ppermute x1, starting transfers between devices, padded_2(): lax.ppermute(lax.slice_in_dim(block, 0, width, axis=dim), axis, backward)  5.15 us
    unnamed x2, other arithmetic  4.04 us
  transfers between devices with their start and end apart: 3, of which 2 were waited for; matrix products, arithmetic and copies ran while one was open for 2% of the time, Pallas kernels for 0%

commit v1 on v0

--- a/solution.py
+++ b/solution.py
@@ -121,7 +121,9 @@
     projected_cross = jnp.dot(normed_cross, qkv_cross, preferred_element_type=jnp.float32)
     q_cross, k_cross, v_cross = split_heads(projected_cross, qk_gain_cross)
     pair = jnp.stack([k_cross.reshape(rows, width), v_cross.reshape(rows, width)])[None]
-    every = lax.all_gather(pair, "stem", axis=0, tiled=True)
+    every = jnp.concatenate(
+        lax.all_to_all(jnp.stack([pair] * lax.axis_size("stem")), "stem", 0, 0), axis=0
+    )
     k_all = every[:, 0].reshape(stem_count, rows, H, HD)
     v_all = every[:, 1].reshape(stem_count, rows, H, HD)
     scores = jnp.einsum(

time: 177 us -> 151 us (0.85)
  the two profiles are of different devices: /device:TPU:1 before, /device:TPU:71 now
where the time goes in v1:
time: 151 us
  waiting for transfers between devices  79.3 us (53%)
  local copies, waits for them, and re-layouts  21.6 us (14%)
  other arithmetic  17.9 us (12%)
  matrix products  17.6 us (12%)
  starting transfers between devices  13.7 us (9%)
    all_to_all x1, waiting for transfers between devices, on_device(): lax.all_to_all(jnp.stack([pair] * lax.axis_size('stem')), 'stem', 0, 0)  69.6 us
    sub x1, matrix products, softmax_rows(): raised = jnp.exp(scores - top)  9.13 us
    ppermute x1, waiting for transfers between devices, padded_2(): lax.ppermute(lax.slice_in_dim(block, 0, width, axis=dim), axis, backward)  8.48 us
    convert_element_type x6, other arithmetic, rounded(): return lax.optimization_barrier(values.astype(jnp.bfloat16))  7.52 us
    unnamed x34, local copies, waits for them, and re-layouts  7.51 us
    ppermute x1, starting transfers between devices, padded_2(): lax.ppermute(lax.slice_in_dim(block, block.shape[dim] - width, None, axis...  6.19 us
    all_to_all x1, starting transfers between devices, on_device(): lax.all_to_all(jnp.stack([pair] * lax.axis_size('stem')), 'stem', 0, 0)  4.96 us
    all_to_all x1, local copies, waits for them, and re-layouts, on_device(): lax.all_to_all(jnp.stack([pair] * lax.axis_size('stem')), 'stem', 0, 0)  3.51 us
  transfers between devices with their start and end apart: 3, of which 3 were waited for; matrix products, arithmetic and copies ran while one was open for 2% of the time, Pallas kernels for 0%

profile of v1, /device:TPU:71, one launch (start us, length us, event | category | flops | bytes accessed | tf_op | source)
XLA Modules:
  0.0 150.6 jit_solution(2018885708322718750)
XLA Ops:
  0.0 2.2 %copy.33 = f32[50,6,1024]{2,1,0:T(8,128)S(1)} copy(f32[50,6,1024]{2,0,1:T(8,128)} %param.11) | data formatting | bytes 2457600 | tf_op args[2]
  2.2 0.3 pad.10
  2.5 1.9 %copy.58 = f32[7,8,6,1024]{3,1,2,0:T(8,128)} copy(f32[7,8,6,1024]{3,2,1,0:T(8,128)S(1)} %bitcast.96) | data formatting | bytes 2752512
  4.4 2.9 %dot_general.34 = f32[6,1024,50]{1,0,2:T(8,128)} reshape(f32[6144,50]{0,1:T(8,128)} %bitcast.97) | data formatting | bytes 2457600 | tf_op jit(solution)/shard_map/dot_general | solution.py:104
  7.3 1.3 convert_reduce_fusion.1
  8.6 1.5 fusion.17
  10.1 2.6 %fusion.23 = f32[8,6,1024]{2,0,1:T(8,128)S(1)} fusion(f32[6,1024,50]{1,0,2:T(8,128)} %dot_general.34, s32[8]{0:T(128)S(1)} %copy-done.11), kind=kOutput, calls=%fused_computation.36 | convolution fusion | flops 29491600 | bytes 1425440 | tf_op jit(solution)/shard_map/dot_general | solution.py:104
  12.7 1.5 fusion.20
  14.3 1.4 fusion.52
  15.6 0.0 copy-start.9
  15.7 0.1 fusion.49
  15.8 0.1 slice.123
  15.8 0.5 copy-done.9
  16.3 0.3 copy.37
  16.6 0.1 multiply_reduce_fusion.4
  16.7 0.3 copy.35
  17.0 0.1 multiply_reduce_fusion.5
  17.1 0.3 multiply_convert_fusion.2
  17.4 0.2 copy.36
  17.6 0.1 fusion.34
  17.7 2.6 %collective-permute-start.1 = (bf16[2,256,512]{1,2,0:T(8,128)(2,1)S(1)}, bf16[2,256,512]{1,2,0:T(8,128)(2,1)S(1)}, u32[]{:S(2)}, u32[]{:S(2)}) collective-permute-start(bf16[2,256,512]{1,2,0:T(8,128)(2,1)S(1)} %get-tuple-element.29), channel_id=1, source_target_pairs={{1,0},{2,1},{3,2},{4,3},{5,4},{6,5},{7,6},{8,7},{9,8},{10,9},{11,1... | collective-permute-start | bytes 1572872 | tf_op jit(solution)/shard_map/ppermute | solution.py:22
  20.3 6.2 %collective-permute-start = (bf16[2,256,512]{1,2,0:T(8,128)(2,1)S(1)}, bf16[2,256,512]{1,2,0:T(8,128)(2,1)}, u32[]{:S(2)}, u32[]{:S(2)}) collective-permute-start(bf16[2,256,512]{1,2,0:T(8,128)(2,1)S(1)} %get-tuple-element.28), channel_id=1, source_target_pairs={{0,1},{1,2},{2,3},{3,4},{4,5},{5,6},{6,7},{7,8},{8,9},{9,10},{10,1... | collective-permute-start | bytes 1572872 | tf_op jit(solution)/shard_map/ppermute | solution.py:19
  26.6 0.6 slice_bitcast_fusion.1
  27.2 1.2 fusion.26
  28.4 8.5 %collective-permute-done.1 = bf16[2,256,512]{1,2,0:T(8,128)(2,1)S(1)} collective-permute-done((bf16[2,256,512]{1,2,0:T(8,128)(2,1)S(1)}, bf16[2,256,512]{1,2,0:T(8,128)(2,1)S(1)}, u32[]{:S(2)}, u32[]{:S(2)}) %collective-permute-start.1) | collective-permute-done | bytes 524320 | tf_op jit(solution)/shard_map/ppermute | solution.py:22
  36.9 1.1 collective-permute-done
  38.0 1.2 pad_maximum_fusion
  39.2 1.1 fusion.50
  40.3 9.1 %fusion.51 = (f32[8,384]{1,0:T(8,128)S(1)}, f32[8,384,896]{2,1,0:T(8,128)}) fusion(pred[384,896]{1,0:T(8,128)(4,1)S(1)} %copy-done.6, bf16[384,8,64]{0,2,1:T(8,128)(2,1)S(1)} %get-tuple-element.42, bf16[896,8,64]{0,2,1:T(8,128)(2,1)} %bitcast.105), kind=kOutput, calls=%fused_computation.99 | convolution fusion | flops 363332480 | bytes 12677120 | tf_op jit(solution)/shard_map/while/body/eval_jaxpr/sub | solution.py:56
  49.5 5.0 %divide_convert_fusion = bf16[8,384,896]{2,1,0:T(8,128)(2,1)S(1)} fusion(f32[8,384,896]{2,1,0:T(8,128)} %get-tuple-element.41, f32[8,384]{1,0:T(8,128)S(1)} %get-tuple-element.40), kind=kLoop, calls=%fused_computation.3 | loop fusion | flops 5505024 | bytes 16527360 | tf_op jit(solution)/shard_map/while/body/eval_jaxpr/convert_element_type | solution.py:28
  54.5 0.0 copy-start.4
  54.5 1.9 %convolution_convert_fusion.1 = bf16[8,64,384]{2,1,0:T(8,128)(2,1)S(1)} fusion(bf16[896,8,64]{0,2,1:T(8,128)(2,1)S(1)} %bitcast.98, bf16[8,384,896]{2,1,0:T(8,128)(2,1)S(1)} %divide_convert_fusion), kind=kOutput, calls=%fused_computation.41 | convolution fusion | flops 352518144 | bytes 6815744 | tf_op jit(solution)/shard_map/while/body/eval_jaxpr/hqk,khd->qhd/dot_general | solution.py:79
  56.4 0.6 fusion.21
  57.1 0.2 convert_reduce_fusion
  57.3 0.3 fusion.13
  57.6 0.4 fusion.16
  58.0 1.2 copy-done.12
  59.2 1.4 fusion.53
  60.7 0.1 slice.122
  60.7 0.1 fusion.48
  60.9 0.2 copy.40
  61.1 0.3 copy.39
  61.3 0.1 multiply_reduce_fusion.2
  61.4 0.1 copy-done.8
  61.5 0.1 multiply_convert_fusion
  61.7 0.1 pad_maximum_fusion.1
  61.8 3.5 %stack.11 = bf16[8,1,2,384,512]{3,4,2,1,0:T(8,128)(2,1)} broadcast(bf16[2,384,512]{1,2,0:T(8,128)(2,1)S(1)} %pad_maximum_fusion.1), dimensions={2,3,4} | broadcast | bytes 7077888 | tf_op jit(solution)/shard_map/stack | solution.py:125
  65.2 5.0 %all-to-all-start = ((bf16[8,1,2,384,512]{3,4,2,1,0:T(8,128)(2,1)}), bf16[8,1,2,384,512]{3,4,2,1,0:T(8,128)(2,1)}, u32[]{:S(2)}, u32[]{:S(2)}) async-start(bf16[8,1,2,384,512]{3,4,2,1,0:T(8,128)(2,1)} %stack.11), calls=%async_computation | async-start | bytes 12582912 | tf_op jit(solution)/shard_map/all_to_all | solution.py:125
  70.2 0.3 copy.38
  70.5 0.1 multiply_reduce_fusion.3
  70.6 0.3 copy-done.7
  70.9 0.1 multiply_convert_fusion.1
  71.0 0.9 convert.8
  72.0 69.6 %all-to-all-done = bf16[8,1,2,384,512]{3,4,2,1,0:T(8,128)(2,1)} async-done(((bf16[8,1,2,384,512]{3,4,2,1,0:T(8,128)(2,1)}), bf16[8,1,2,384,512]{3,4,2,1,0:T(8,128)(2,1)}, u32[]{:S(2)}, u32[]{:S(2)}) %all-to-all-start) | async-done | bytes 6291488 | tf_op jit(solution)/shard_map/all_to_all | solution.py:125
  141.6 3.5 %copy.68 = bf16[8,1,2,384,512]{3,4,0,2,1:T(8,128)(2,1)S(1)} copy(bf16[8,1,2,384,512]{3,4,2,1,0:T(8,128)(2,1)} %all-to-all-done) | data formatting | bytes 12582912 | tf_op jit(solution)/shard_map/all_to_all | solution.py:125
  145.1 0.7 fusion.47
  145.8 0.4 copy-done.5
  146.3 1.0 multiply_reduce_fusion.1
  147.3 0.1 fusion.32
  147.4 0.8 multiply_reduce_fusion
  148.2 0.4 copy-done.14
  148.6 0.6 convolution_convert_fusion
  149.2 0.2 copy-done.3
  149.4 1.2 fusion.33
  (35 shorter events, 0.2 us)
Async XLA Ops:
  0.0 14.2 %copy-start = (bf16[1024,1536]{1,0:T(8,128)(2,1)S(1)}, bf16[1024,1536]{1,0:T(8,128)(2,1)}, u32[]{:S(2)}) copy-start(bf16[1024,1536]{1,0:T(8,128)(2,1)} %param.12) | copy-start | bytes 9437188
  4.4 5.7 %copy-start.11 = (s32[8]{0:T(128)S(1)}, s32[8]{0:T(128)}, u32[]{:S(2)}) copy-start(s32[8]{0:T(128)} %param.10) | copy-start | bytes 100
  15.6 0.7 copy-start.9
  17.4 9.2 %copy-start.10 = (f32[2,64]{1,0:T(2,128)S(1)}, f32[2,64]{1,0:T(2,128)}, u32[]{:S(2)}) copy-start(f32[2,64]{1,0:T(2,128)} %param.17) | copy-start | bytes 1540
  17.7 19.1 %collective-permute-start.1 = (bf16[2,256,512]{1,2,0:T(8,128)(2,1)S(1)}, bf16[2,256,512]{1,2,0:T(8,128)(2,1)S(1)}, u32[]{:S(2)}, u32[]{:S(2)}) collective-permute-start(bf16[2,256,512]{1,2,0:T(8,128)(2,1)S(1)} %get-tuple-element.29), channel_id=1, source_target_pairs={{1,0},{2,1},{3,2},{4,3},{5,4},{6,5},{7,6},{8,7},{9,8},{10,9},{11,1... | collective-permute-start | bytes 1572872 | tf_op jit(solution)/shard_map/ppermute | solution.py:22
  20.3 17.7 %collective-permute-start = (bf16[2,256,512]{1,2,0:T(8,128)(2,1)S(1)}, bf16[2,256,512]{1,2,0:T(8,128)(2,1)}, u32[]{:S(2)}, u32[]{:S(2)}) collective-permute-start(bf16[2,256,512]{1,2,0:T(8,128)(2,1)S(1)} %get-tuple-element.28), channel_id=1, source_target_pairs={{0,1},{1,2},{2,3},{3,4},{4,5},{5,6},{6,7},{7,8},{8,9},{9,10},{10,1... | collective-permute-start | bytes 1572872 | tf_op jit(solution)/shard_map/ppermute | solution.py:19
  39.2 1.1 copy-start.6
  54.5 1.9 %copy-start.4 = (bf16[1,384,1024]{2,1,0:T(8,128)(2,1)S(1)}, bf16[1,384,1024]{2,1,0:T(8,128)(2,1)}, u32[]{:S(2)}) copy-start(bf16[1,384,1024]{2,1,0:T(8,128)(2,1)} %param.9) | copy-start | bytes 2359300
  54.5 1.9 %copy-start.13 = (bf16[512,1024]{1,0:T(8,128)(2,1)S(1)}, bf16[512,1024]{1,0:T(8,128)(2,1)}, u32[]{:S(2)}) copy-start(bf16[512,1024]{1,0:T(8,128)(2,1)} %param.13) | copy-start | bytes 3145732
  57.1 3.6 %copy-start.2 = (bf16[384,1024]{1,0:T(8,128)(2,1)}, bf16[384,1024]{1,0:T(8,128)(2,1)S(1)}, u32[]{:S(2)}) copy-start(bf16[384,1024]{1,0:T(8,128)(2,1)S(1)} %fusion.21) | copy-start | bytes 2359300
  57.1 2.2 %copy-start.12 = (bf16[1024,1536]{1,0:T(8,128)(2,1)S(1)}, bf16[1024,1536]{1,0:T(8,128)(2,1)}, u32[]{:S(2)}) copy-start(bf16[1024,1536]{1,0:T(8,128)(2,1)} %param.15) | copy-start | bytes 9437188
  60.8 0.7 copy-start.8
  65.2 76.4 %all-to-all-start = ((bf16[8,1,2,384,512]{3,4,2,1,0:T(8,128)(2,1)}), bf16[8,1,2,384,512]{3,4,2,1,0:T(8,128)(2,1)}, u32[]{:S(2)}, u32[]{:S(2)}) async-start(bf16[8,1,2,384,512]{3,4,2,1,0:T(8,128)(2,1)} %stack.11), calls=%async_computation | async-start | bytes 12582912 | tf_op jit(solution)/shard_map/all_to_all | solution.py:125
  70.2 0.7 copy-start.7
  145.1 1.1 copy-start.5
  147.4 1.2 copy-start.14
  148.2 1.2 copy-start.3
  148.2 2.4 %copy-start.1 = (bf16[1024,1536]{1,0:T(8,128)(2,1)S(1)}, bf16[1024,1536]{1,0:T(8,128)(2,1)}, u32[]{:S(2)}) copy-start(bf16[1024,1536]{1,0:T(8,128)(2,1)} %param.12) | copy-start | bytes 9437188
